TPU v7x, 128 devices: a whole 4x4x4 slice. The times are simulated.
128 devices in a mesh: arc: 4 (over z), nr: 8 (over y_lo, x), nc: 4 (over y_hi, core).
Axes of the slice: x: 4, y: 4 (y_hi: 2, y_lo: 2; y = y_hi * 2 + y_lo), z: 4, core: 2. Of those that a mesh axis runs over, the one named last changes fastest.
Arguments:
- design: float32 [2048, 16384], P('arc', ('nr', 'nc')), may hold values from -6 to 6
- root_tiles: float32 [4, 512, 512], P('arc'), may hold values from -0.25 to 0.25
- row_weights: float32 [2048], P('arc'), may hold values from 0.25 to 4
- prior_sd: float32 [16384], P(('nr', 'nc')), may hold values from 0.1 to 1
- probe_signs: int32 [16384, 128], P(('nr', 'nc')), may hold values from -1 to 1, as said below
Outputs:
- normals: float32 [8, 2048, 8, 2048], P('nr', 'arc', None, 'nc')
- probe_products: float32 [8, 2048, 128], P('nr', ('arc', 'nc'))
- design_probe: float32 [2048, 128], P(('arc', 'nr', 'nc'))
Inputs may be any that keep to these rules, and one draw needn't show every extreme that they name: `probe_signs`: every entry is -1 or 1.
All inputs are finite; a program needn't handle non-finite values.
Results may differ from a plain program's by a relative error of at most 0.000073.
Values sent between devices are 32-bit elements; how exact they have to be, the bound alone decides.
No kernel may reach another device: no remote copies, remote signals or barrier semaphores. Data moves between devices by JAX's collectives and lax.ppermute only.
A program may use at most 128 MiB of HBM per device.

v0:
```python
import jax
import jax.numpy as jnp
from jax import lax
from jax.sharding import PartitionSpec as P

P_SIZE = 16384


def per_device(design, root_tiles, row_weights, prior_sd, probe_signs):
    row_count, span_width = design.shape
    arc_count = lax.axis_size("arc")
    grid_rows = lax.axis_size("nr")
    total_rows = row_count * arc_count
    tile_count, tile_size, _ = root_tiles.shape
    whitened = jnp.einsum(
        "bij,bjk->bik",
        root_tiles,
        design.reshape(tile_count, tile_size, span_width),
        precision=lax.Precision.HIGHEST,
    ).reshape(row_count, span_width)
    scaled = whitened * (row_weights / total_rows)[:, None]
    row_panel = lax.all_gather(scaled, "nc", axis=1, tiled=True)
    slab_rows = row_panel.shape[1] // arc_count
    row_slices = lax.all_to_all(row_panel, "arc", split_axis=1, concat_axis=0, tiled=True)
    initial = jnp.zeros((slab_rows, grid_rows, span_width), jnp.float32)
    col_pieces = lax.all_gather(whitened[None], ("arc", "nr"), axis=0, tiled=True)

    def add_piece(step_index, totals):
        arc_index = step_index // grid_rows
        grid_row = step_index % grid_rows
        row_part = lax.dynamic_slice_in_dim(row_slices, arc_index * row_count, row_count, 0)
        col_part = lax.dynamic_index_in_dim(col_pieces, step_index, 0, keepdims=False)
        contribution = jnp.einsum(
            "rp,rc->pc",
            row_part,
            col_part,
            precision=lax.Precision.HIGHEST,
            preferred_element_type=jnp.float32,
        )
        current = lax.dynamic_index_in_dim(totals, grid_row, 1, keepdims=False)
        return lax.dynamic_update_index_in_dim(totals, current + contribution, grid_row, 1)

    gram_block = lax.fori_loop(0, col_pieces.shape[0], add_piece, initial)
    gram_block = gram_block.reshape(slab_rows, grid_rows * span_width)
    normals_out = gram_block.reshape(1, slab_rows, grid_rows, span_width)
    probes = probe_signs.astype(jnp.float32) * prior_sd[:, None]
    probe_cols = lax.all_gather(probes, "nr", axis=0, tiled=True)
    applied_part = jnp.dot(
        gram_block, probe_cols, precision=lax.Precision.HIGHEST, preferred_element_type=jnp.float32
    )
    applied_own = lax.psum_scatter(applied_part, "nc", scatter_dimension=0, tiled=True)
    probe_panel = lax.all_gather(applied_own, ("arc", "nc"), axis=0, tiled=True)
    own_probes = lax.dynamic_slice_in_dim(
        probe_panel, lax.axis_index("nc") * span_width, span_width, 0
    )
    row_part = whitened
    design_probe = lax.psum_scatter(
        jnp.dot(
            row_part,
            own_probes,
            precision=lax.Precision.HIGHEST,
            preferred_element_type=jnp.float32,
        )
        * P_SIZE ** (-0.5),
        ("nr", "nc"),
        scatter_dimension=0,
        tiled=True,
    )
    return (normals_out, applied_own[None], design_probe)


def solution(mesh):
    in_specs = (
        P("arc", ("nr", "nc")),
        P("arc", None, None),
        P("arc"),
        P(("nr", "nc")),
        P(("nr", "nc"), None),
    )
    out_specs = (
        P("nr", "arc", None, "nc"),
        P("nr", ("arc", "nc"), None),
        P(("arc", "nr", "nc"), None),
    )
    return jax.shard_map(
        per_device, mesh=mesh, in_specs=in_specs, out_specs=out_specs, check_vma=False
    )
```

profile of v0, /device:TPU:0, one launch (start us, length us, event | category | flops | bytes accessed | tf_op | source)
XLA Modules:
  0.0 887.8 jit_solution(11152165098740075711)
XLA Ops:
  8.4 4.4 broadcast_multiply_fusion
  13.6 40.4 %all-gather.6.cloned.1.call-done = f32[512,2048]{1,0:T(8,128)} async-done(((f32[512,512]{1,0:T(8,128)}), f32[512,2048]{1,0:T(8,128)}) %all-gather.6.cloned.1.call-update) | async-done | bytes 4194320 | tf_op jit(solution)/shard_map/all_gather | solution.py:22
  54.0 4.8 copy.20
  58.8 4.9 all-to-all-start
  64.9 396.7 %all-to-all-done = f32[512,4,512]{2,0,1:T(8,128)} async-done(((f32[512,4,512]{2,0,1:T(8,128)}), f32[512,4,512]{2,0,1:T(8,128)}, u32[]{:S(2)}, u32[]{:S(2)}) %all-to-all-start) | async-done | bytes 4194336 | tf_op jit(solution)/shard_map/all_to_all | solution.py:24
  461.5 4.3 broadcast_in_dim.19
  465.8 182.6 %while.15 = (s32[]{:T(128)}, f32[512,8,512]{2,0,1:T(8,128)}, f32[2048,512]{1,0:T(8,128)}, f32[32,512,512]{2,1,0:T(8,128)}, s32[]{:T(128)}, /*index=5*/s32[]{:T(1...) while((s32[]{:T(128)}, f32[512,8,512]{2,0,1:T(8,128)}, ...), condition=%wide.region_1.2_spmd, body=%wide.region_0.1_spmd.sunk | while | flops 1610874880 | bytes 6292292 | solution.py:43
  465.8 1.3 constant_dynamic-slice_fusion.2
  467.1 4.4 fusion.20
  471.5 1.3 constant_dynamic-slice_fusion.2
  472.9 4.4 fusion.20
  478.5 4.4 fusion.20
  484.2 4.4 fusion.20
  490.0 4.4 fusion.20
  495.7 4.4 fusion.20
  501.4 4.4 fusion.20
  507.0 4.4 fusion.20
  512.8 4.4 fusion.20
  518.5 4.4 fusion.20
  524.2 4.4 fusion.20
  529.9 4.4 fusion.20
  535.6 4.4 fusion.20
  541.3 4.4 fusion.20
  547.0 4.4 fusion.20
  552.7 4.4 fusion.20
  558.5 4.4 fusion.20
  564.2 4.4 fusion.20
  569.9 4.4 fusion.20
  575.5 4.4 fusion.20
  581.3 4.4 fusion.20
  587.0 4.4 fusion.20
  592.7 4.4 fusion.20
  598.4 4.4 fusion.20
  604.1 4.4 fusion.20
  609.8 4.4 fusion.20
  615.5 4.4 fusion.20
  621.2 4.4 fusion.20
  626.9 4.4 fusion.20
  632.7 4.4 fusion.20
  638.3 4.4 fusion.20
  644.0 4.4 fusion.20
  648.5 9.1 %copy.15 = f32[512,8,512]{0,2,1:T(8,128)} copy(f32[512,8,512]{2,0,1:T(8,128)} %get-tuple-element.116) | data formatting | bytes 16777216 | tf_op jit(solution)/shard_map/while | solution.py:43
  657.6 16.6 %fusion.10 = f32[512,128]{1,0:T(8,128)} fusion(f32[512,4096]{0,1:T(8,128)} %bitcast.37, f32[4096,128]{1,0:T(8,128)} %all-gather.8.cloned.1.call-done), kind=kOutput, calls=%fused_computation.18 | convolution fusion | flops 3221225472 | bytes 10747904 | tf_op jit(solution)/shard_map/dot_general | solution.py:48
  674.3 24.2 %reduce-scatter.3.cloned.1.call-done = f32[128,128]{1,0:T(8,128)} async-done(((f32[512,128]{1,0:T(8,128)}), f32[128,128]{1,0:T(8,128)}) %reduce-scatter.3.cloned.1.call-update) | async-done | bytes 65552 | tf_op jit(solution)/shard_map/reduce_scatter | solution.py:51
  698.8 46.8 %all-gather.10.cloned.1.call-done = f32[2048,128]{1,0:T(8,128)} async-done(((f32[128,128]{1,0:T(8,128)}), f32[2048,128]{1,0:T(8,128)}) %all-gather.10.cloned.1.call-update) | async-done | bytes 1048592 | tf_op jit(solution)/shard_map/all_gather | solution.py:52
  745.6 2.6 convolution_multiply_fusion
  748.3 11.7 %copy.19 = f32[512,8,512]{2,1,0:T(8,128)} copy(f32[512,8,512]{2,0,1:T(8,128)} %get-tuple-element.116) | data formatting | bytes 16777216 | tf_op jit(solution)/shard_map/while | solution.py:43
  760.0 120.9 %reduce-scatter.5.cloned.1.call-done = f32[16,128]{1,0:T(8,128)} async-done(((f32[512,128]{1,0:T(8,128)}), f32[16,128]{1,0:T(8,128)}) %reduce-scatter.5.cloned.1.call-update) | async-done | bytes 8208 | tf_op jit(solution)/shard_map/reduce_scatter | solution.py:57
  (56 shorter events, 42.3 us)
Async XLA Ops:
  7.2 1.2 copy-start
  7.2 46.8 %all-gather.6.cloned.1.call-start = ((), (), s32[]{:S(2)}) async-start(), calls=%async_computation.3 | async-start | bytes 5242880 | tf_op jit(solution)/shard_map/all_gather | solution.py:22
  12.8 448.7 %all-gather.12.cloned.1.call-start = ((), (), s32[]{:S(2)}) async-start(), calls=%async_computation.8 | async-start | bytes 34603008 | tf_op jit(solution)/shard_map/all_gather | solution.py:26
  54.0 9.8 %copy-start.3 = (s32[512,128]{1,0:T(8,128)S(1)}, s32[512,128]{1,0:T(8,128)}, u32[]{:S(2)}) copy-start(s32[512,128]{1,0:T(8,128)} %param.11) | copy-start | bytes 786436
  54.0 9.8 %copy-start.4 = (f32[512]{0:T(512)S(1)}, f32[512]{0:T(512)}, u32[]{:S(2)}) copy-start(f32[512]{0:T(512)} %param.10) | copy-start | bytes 6148
  58.8 402.7 %all-to-all-start = ((f32[512,4,512]{2,0,1:T(8,128)}), f32[512,4,512]{2,0,1:T(8,128)}, u32[]{:S(2)}, u32[]{:S(2)}) async-start(f32[512,4,512]{2,0,1:T(8,128)} %bitcast.38), calls=%async_computation | async-start | bytes 8388608 | tf_op jit(solution)/shard_map/all_to_all | solution.py:24
  63.7 593.9 %all-gather.8.cloned.1.call-start = ((), (), s32[]{:S(2)}) async-start(), calls=%async_computation.4 | async-start | bytes 2359296 | tf_op jit(solution)/shard_map/all_gather | solution.py:47
  64.6 633.9 %reduce-scatter.3.cloned.1.call-start = ((), (), s32[]{:S(2)}) async-start(), calls=%async_computation.5 | async-start | bytes 327680 | tf_op jit(solution)/shard_map/reduce_scatter | solution.py:51
  657.6 88.0 %copy-start.2 = (f32[512,512]{1,0:T(8,128)S(1)}, f32[512,512]{1,0:T(8,128)}, u32[]{:S(2)}) copy-start(f32[512,512]{1,0:T(8,128)} %get-tuple-element.126) | copy-start | bytes 3145732
  674.2 71.4 %all-gather.10.cloned.1.call-start = ((), (), s32[]{:S(2)}) async-start(), calls=%async_computation.6 | async-start | bytes 1114112 | tf_op jit(solution)/shard_map/all_gather | solution.py:52
  698.5 182.4 %reduce-scatter.5.cloned.1.call-start = ((), (), s32[]{:S(2)}) async-start(), calls=%async_computation.7 | async-start | bytes 270336 | tf_op jit(solution)/shard_map/reduce_scatter | solution.py:57
  748.3 132.6 %copy-start.1 = (f32[512,512]{1,0:T(8,128)S(1)}, f32[512,512]{1,0:T(8,128)}, u32[]{:S(2)}) copy-start(f32[512,512]{1,0:T(8,128)} %param.7) | copy-start | bytes 3145732
Sparse Core Ops, SparseCore 0:
  12.9 40.9 all-gather.5
  55.6 364.3 all-gather.11
  421.6 37.4 all-gather.7
  674.4 24.0 reduce-scatter.2
  701.4 44.2 all-gather.9
  748.4 132.4 reduce-scatter.4
where the time goes:
time: 890 us; the launch traced here: 888 us
  waiting for transfers between devices  630 us (71%)
  matrix products  164 us (18%)
  local copies, waits for them, and re-layouts  71.8 us (8%)
  between operations  14.2 us (2%)
    all_to_all x1, waiting for transfers between devices, per_device(): lax.all_to_all(row_panel, 'arc', split_axis=1, concat_axis=0, tiled=True)  397 us
    dot_general x32, matrix products, add_piece(): jnp.einsum('rp,rc->pc', row_part, col_part, precision=lax.Precision.HIGHE...  141 us
    reduce_scatter x1, waiting for transfers between devices, per_device(): lax.psum_scatter(jnp.dot(row_part, own_probes, precision=lax.Precision.HI...  121 us
    all_gather x1, waiting for transfers between devices, per_device(): probe_panel = lax.all_gather(applied_own, ('arc', 'nc'), axis=0, tiled=True)  46.8 us
    dynamic_slice x32, local copies, waits for them, and re-layouts, add_piece(): current = lax.dynamic_index_in_dim(totals, grid_row, 1, keepdims=False)  41.4 us
    all_gather x1, waiting for transfers between devices, per_device(): row_panel = lax.all_gather(scaled, 'nc', axis=1, tiled=True)  40.4 us
    reduce_scatter x1, waiting for transfers between devices, per_device(): lax.psum_scatter(applied_part, 'nc', scatter_dimension=0, tiled=True)  24.2 us
    while x2, local copies, waits for them, and re-layouts, per_device(): gram_block = lax.fori_loop(0, col_pieces.shape[0], add_piece, initial)  20.8 us
  transfers between devices with their start and end apart: 7, of which 5 were waited for; matrix products, arithmetic and copies ran while one was open for 24% of the time, Pallas kernels for 0%

commit v1 on v0

v1 whole, which is shorter than its diff:
```python
import jax
import jax.numpy as jnp
from jax import lax
from jax.experimental import pallas as pl
from jax.experimental.pallas import tpu as pltpu
from jax.sharding import Mesh, PartitionSpec as P

P_SIZE = 16384
ROWS = 2048
TILE = 512
F32 = jnp.float32
BF16 = jnp.bfloat16


def split(x):
    hi = x.astype(BF16)
    lo = (x - hi.astype(F32)).astype(BF16)
    return hi, lo


def dot(a, b):
    return jnp.dot(a, b, preferred_element_type=F32)


def dot3(a, b):
    ah, al = a
    bh, bl = b
    return dot(ah, bh) + (dot(ah, bl) + dot(al, bh))


def whiten_kernel(design_ref, root_ref, weight_ref, sd_ref, sign_ref, w_ref, st_ref, u_ref):
    w = dot3(split(root_ref[0]), split(design_ref[...]))
    w_ref[...] = w
    st_ref[...] = w.T * (weight_ref[...] * (1.0 / ROWS))
    wh, wl = split(w * sd_ref[...])
    signs = sign_ref[...].astype(F32).astype(BF16)
    u_ref[...] = dot(wh, signs) + dot(wl, signs)


def whiten(design, root, weights, sd, signs):
    return pl.pallas_call(
        whiten_kernel,
        out_shape=(
            jax.ShapeDtypeStruct((TILE, TILE), F32),
            jax.ShapeDtypeStruct((TILE, TILE), F32),
            jax.ShapeDtypeStruct((TILE, 128), F32),
        ),
        name="whiten",
    )(design, root, weights.reshape(1, TILE), sd.reshape(1, TILE), signs)


def gram_first_kernel(where_ref, t0, t1, t2, t3, a_ref, g_ref, hi_ref, lo_ref, acc):
    col, j = pl.program_id(0), pl.program_id(1)

    @pl.when(col == 0)
    def _():
        for i, t in enumerate((t0, t1, t2, t3)):

            @pl.when(j == i)
            def _():
                hi, lo = split(t[...])
                hi_ref[i] = hi
                lo_ref[i] = lo

    part = dot3((hi_ref[j], lo_ref[j]), split(a_ref[0, 0]))

    @pl.when(j == 0)
    def _():
        acc[...] = part

    @pl.when(j > 0)
    def _():
        acc[...] += part

    @pl.when(j == 3)
    def _():
        g_ref[0] = acc[...]


def gram_first(where, parts, gathered):
    whole = pl.BlockSpec((TILE, TILE), lambda i, j, w: (0, 0))
    kept = pl.BlockSpec((4, TILE, TILE), lambda i, j, w: (0, 0, 0))
    return pl.pallas_call(
        gram_first_kernel,
        grid_spec=pltpu.PrefetchScalarGridSpec(
            num_scalar_prefetch=1,
            grid=(4, 4),
            in_specs=[whole] * 4
            + [pl.BlockSpec((1, 1, TILE, TILE), lambda i, j, w: (w[0] ^ j, i, 0, 0))],
            out_specs=(
                pl.BlockSpec((1, TILE, TILE), lambda i, j, w: (i, 0, 0)),
                kept,
                kept,
            ),
            scratch_shapes=[pltpu.VMEM((TILE, TILE), F32)],
        ),
        out_shape=(
            jax.ShapeDtypeStruct((4, TILE, TILE), F32),
            jax.ShapeDtypeStruct((4, TILE, TILE), BF16),
            jax.ShapeDtypeStruct((4, TILE, TILE), BF16),
        ),
        compiler_params=pltpu.CompilerParams(vmem_limit_bytes=56 << 20),
        name="gram_first",
    )(where, *parts, gathered)


def gram_last_kernel(where_ref, hi_ref, lo_ref, first_ref, a_ref, out_ref, acc, held, sems):
    col, j = pl.program_id(0), pl.program_id(1)
    part = dot3((hi_ref[j], lo_ref[j]), split(a_ref[0, 0]))

    @pl.when(j == 0)
    def _():
        acc[...] = part

    @pl.when(j > 0)
    def _():
        acc[...] += part

    own = where_ref[1] * 4 + col
    other = (1 - where_ref[1]) * 4 + col

    @pl.when(j == 0)
    def _():
        for l in range(4):
            lanes = pl.ds(l * 128, 128)
            held[l, pl.ds(own, TILE, stride=8), :] = first_ref[0, :, lanes]

    @pl.when(j == 3)
    def _():
        for l in range(4):
            lanes = pl.ds(l * 128, 128)
            held[l, pl.ds(other, TILE, stride=8), :] = acc[:, lanes]

    @pl.when((j == 3) & (col == 3))
    def _():
        copies = [
            pltpu.make_async_copy(held.at[l], out_ref.at[:, pl.ds(l * 128, 128)], sems.at[l])
            for l in range(4)
        ]
        for copy in copies:
            copy.start()
        for copy in copies:
            copy.wait()


def gram_last(where, hi, lo, first, gathered):
    kept = pl.BlockSpec((4, TILE, TILE), lambda i, j, w: (0, 0, 0))
    return pl.pallas_call(
        gram_last_kernel,
        grid_spec=pltpu.PrefetchScalarGridSpec(
            num_scalar_prefetch=1,
            grid=(4, 4),
            in_specs=[
                kept,
                kept,
                pl.BlockSpec((1, TILE, TILE), lambda i, j, w: (i, 0, 0)),
                pl.BlockSpec((1, 1, TILE, TILE), lambda i, j, w: (w[0] ^ j, i, 0, 0)),
            ],
            out_specs=pl.BlockSpec(memory_space=pl.ANY),
            scratch_shapes=[
                pltpu.VMEM((TILE, TILE), F32),
                pltpu.VMEM((4, TILE * 8, 128), F32),
                pltpu.SemaphoreType.DMA((4,)),
            ],
        ),
        out_shape=jax.ShapeDtypeStruct((TILE * 8, TILE), F32),
        compiler_params=pltpu.CompilerParams(vmem_limit_bytes=56 << 20),
        name="gram_last",
    )(where, hi, lo, first, gathered)


def swap(x, axis, size=2, bit=1):
    return lax.ppermute(x, axis, [(i, i ^ bit) for i in range(size)])


def transpose_devices(x):
    return lax.ppermute(
        x, ("z", "yh", "k"), [(z * 4 + c, c * 4 + z) for z in range(4) for c in range(4)]
    )


def halve(x, axis, size=2, bit=1):
    mine = (lax.axis_index(axis) // bit) % 2
    half = x.shape[0] // 2
    keep = lax.dynamic_slice_in_dim(x, mine * half, half, 0)
    send = lax.dynamic_slice_in_dim(x, (1 - mine) * half, half, 0)
    return keep + swap(send, axis, size, bit)


def probe_chain(w, st, u):
    for axis, size, bit in (("k", 2, 1), ("yh", 2, 1), ("yl", 2, 1), ("x", 4, 1), ("x", 4, 2)):
        u = u + swap(u, axis, size, bit)
    applied = jnp.dot(st, u, precision=lax.Precision.HIGH, preferred_element_type=F32)
    for bit in (1, 2):
        applied = applied + swap(applied, "z", 4, bit)
    piece = lax.dynamic_slice_in_dim(applied, lax.axis_index("z") * 128, 128, 0)
    products = transpose_devices(piece)
    share = jnp.dot(w, applied, precision=lax.Precision.HIGH, preferred_element_type=F32)
    share = share * P_SIZE ** (-0.5)
    for axis, size, bit in (("yl", 2, 1), ("x", 4, 2), ("x", 4, 1), ("yh", 2, 1), ("k", 2, 1)):
        share = halve(share, axis, size, bit)
    return products, share


def per_device(design, root_tiles, row_weights, prior_sd, probe_signs):
    where = jnp.stack([lax.axis_index("yh") * 2 + lax.axis_index("k"), lax.axis_index("yl")])
    where = where.astype(jnp.int32)
    w, st, u = whiten(design, root_tiles, row_weights, prior_sd, probe_signs)
    own = lax.all_gather(w, ("z", "x"), axis=0, tiled=True)
    other = lax.all_gather(swap(w, "yl"), ("z", "x"), axis=0, tiled=True)
    t0 = transpose_devices(st)
    t2 = swap(t0, "yh")
    t1 = swap(t0, "k")
    t3 = swap(t2, "k")
    first, hi, lo = gram_first(where, (t0, t1, t2, t3), own.reshape(4, 4, TILE, TILE))
    normals = gram_last(where, hi, lo, first, other.reshape(4, 4, TILE, TILE))
    products, share = probe_chain(w, st, u)
    return normals.reshape(1, TILE, 8, TILE), products[None], share


def solution(mesh):
    split_mesh = Mesh(mesh.devices.reshape(4, 2, 4, 2, 2), ("z", "yl", "x", "yh", "k"))
    nr, nc = ("yl", "x"), ("yh", "k")
    in_specs = (
        P("z", nr + nc),
        P("z", None, None),
        P("z"),
        P(nr + nc),
        P(nr + nc, None),
    )
    out_specs = (
        P(nr, "z", None, nc),
        P(nr, ("z",) + nc, None),
        P(("z",) + nr + nc, None),
    )
    return jax.shard_map(
        per_device, mesh=split_mesh, in_specs=in_specs, out_specs=out_specs, check_vma=False
    )
```

time: 890 us -> 310 us (0.35)
  waiting for transfers between devices: 630 us -> 200 us
  matrix products: 164 us -> 2.4 us
  local copies, waits for them, and re-layouts: 71.8 us -> 3.31 us
  Pallas kernels: 0 us -> 58.4 us
  starting transfers between devices: 5.5 us -> 26.1 us
    all_to_all x1 -> x0, waiting for transfers between devices: 397 us -> none  [per_device(): lax.all_to_all(row_panel, 'arc', split_axis=1, concat_axis=0, tiled=True)]
    dot_general x35 -> x2, matrix products: 164 us -> 2.4 us  [the longest x1 1.8 us: probe_chain(): jnp.dot(st, u, precision=lax.Precision.HIGH, preferred_element_type=F32)]
    reduce_scatter x2 -> x0, waiting for transfers between devices: 145 us -> none  [the longest x1 121 us: per_device(): lax.psum_scatter(jnp.dot(row_part, own_probes, precision=lax.Precision.HI...]
    ppermute x0 -> x18, waiting for transfers between devices: none -> 144 us  [the longest x16 144 us: swap(): return lax.ppermute(x, axis, [(i, i ^ bit) for i in range(size)])]
    pallas_call x0 -> x3, Pallas kernels: none -> 58.4 us  [the longest x1 27.7 us: gram_last(): pl.pallas_call(gram_last_kernel, grid_spec=pltpu.PrefetchScalarGridSpec(n...]
    dynamic_slice x32 -> x6, local copies, waits for them, and re-layouts: 41.4 us -> 0.06 us  [the longest x5 0.05 us: halve(): send = lax.dynamic_slice_in_dim(x, (1 - mine) * half, half, 0)]
    all_gather x4 -> x2, waiting for transfers between devices: 87.3 us -> 56.4 us  [the longest x1 56.4 us: per_device(): other = lax.all_gather(swap(w, 'yl'), ('z', 'x'), axis=0, tiled=True)]
    ppermute x0 -> x18, starting transfers between devices: none -> 26 us  [the longest x16 23.4 us: swap(): return lax.ppermute(x, axis, [(i, i ^ bit) for i in range(size)])]
  transfers between devices with their start and end apart: 7 -> 20, of which waited for: 5 -> 14; matrix products, arithmetic and copies ran while one was open for 24% -> 2% of each run, Pallas kernels for 0% -> 9%
where the time goes in v1:
time: 310 us; the launch traced here: 309 us
  waiting for transfers between devices  200 us (65%)
  Pallas kernels  58.4 us (19%)
  starting transfers between devices  26.1 us (8%)
  between operations  14.3 us (5%)
  other arithmetic  4.37 us (1%)
  local copies, waits for them, and re-layouts  3.31 us (1%)
    ppermute x16, waiting for transfers between devices, swap(): return lax.ppermute(x, axis, [(i, i ^ bit) for i in range(size)])  144 us
    all_gather x1, waiting for transfers between devices, per_device(): other = lax.all_gather(swap(w, 'yl'), ('z', 'x'), axis=0, tiled=True)  56.4 us
    pallas_call x1, Pallas kernels, gram_last(): pl.pallas_call(gram_last_kernel, grid_spec=pltpu.PrefetchScalarGridSpec(n...  27.7 us
    pallas_call x1, Pallas kernels, gram_first(): pl.pallas_call(gram_first_kernel, grid_spec=pltpu.PrefetchScalarGridSpec(...  26.3 us
    ppermute x16, starting transfers between devices, swap(): return lax.ppermute(x, axis, [(i, i ^ bit) for i in range(size)])  23.4 us
  transfers between devices with their start and end apart: 20, of which 14 were waited for; matrix products, arithmetic and copies ran while one was open for 2% of the time, Pallas kernels for 9%

profile of v1, /device:TPU:0, one launch (start us, length us, event | category | flops | bytes accessed | tf_op | source)
XLA Modules:
  0.0 308.9 jit_solution(5258451757991079648)
XLA Ops:
  7.2 0.0 all-gather.3.cloned.1.call-start
  7.2 4.3 %whiten.1 = (f32[512,512]{1,0:T(8,128)}, f32[512,512]{1,0:T(8,128)}, f32[512,128]{1,0:T(8,128)}) custom-call(f32[512,512]{1,0:T(8,128)} %design_ref.1, f32[1,512,512]{2,1,0:T(8,128)} %root_ref.1, f32[1,512]{1,0:T(1,128)} %bitcast.15, f32[1,512]{1,0:T(1,128)} %bitcast.16, s32[512,128]{1,0:T(8,128)} %sign_ref.1), custom_call_target="tpu_custom_call" | custom-call | tf_op jit(solution)/shard_map/whiten/pallas_call | solution.py:41
  11.5 0.0 all-gather.3.cloned.1.call-update
  11.5 0.0 all-gather.5.cloned.1.call-start
  11.6 1.8 collective-permute-start.4
  13.3 23.4 %collective-permute-done.4 = f32[512,512]{1,0:T(8,128)S(1)} collective-permute-done((f32[512,512]{1,0:T(8,128)}, f32[512,512]{1,0:T(8,128)S(1)}, u32[]{:S(2)}, u32[]{:S(2)}) %collective-permute-start.4) | collective-permute-done | bytes 1048608 | tf_op jit(solution)/shard_map/ppermute | solution.py:173
  36.7 1.0 copy-done.5
  37.7 0.1 collective-permute-start.5
  37.8 1.7 collective-permute-done.5
  39.5 1.0 add.94
  40.5 3.4 %collective-permute-start.6 = (f32[512,128]{1,0:T(8,128)S(1)}, f32[512,128]{1,0:T(8,128)S(1)}, u32[]{:S(2)}, u32[]{:S(2)}) collective-permute-start(f32[512,128]{1,0:T(8,128)S(1)} %add.94), channel_id=1, source_target_pairs={{0,2},{2,0},{1,3},{3,1},{4,6},{6,4},{5,7},{7,5},{8,10},{10,8},{9,1... | collective-permute-start | bytes 786440 | tf_op jit(solution)/shard_map/ppermute | solution.py:173
  43.9 6.6 %collective-permute-done.6 = f32[512,128]{1,0:T(8,128)S(1)} collective-permute-done((f32[512,128]{1,0:T(8,128)S(1)}, f32[512,128]{1,0:T(8,128)S(1)}, u32[]{:S(2)}, u32[]{:S(2)}) %collective-permute-start.6) | collective-permute-done | bytes 262176 | tf_op jit(solution)/shard_map/ppermute | solution.py:173
  50.6 1.7 collective-permute-start.7
  52.3 6.0 %collective-permute-done.7 = f32[512,128]{1,0:T(8,128)S(1)} collective-permute-done((f32[512,128]{1,0:T(8,128)S(1)}, f32[512,128]{1,0:T(8,128)S(1)}, u32[]{:S(2)}, u32[]{:S(2)}) %collective-permute-start.7) | collective-permute-done | bytes 262176 | tf_op jit(solution)/shard_map/ppermute | solution.py:173
  58.3 1.5 collective-permute-start.8
  59.8 12.6 %collective-permute-done.8 = f32[512,128]{1,0:T(8,128)S(1)} collective-permute-done((f32[512,128]{1,0:T(8,128)S(1)}, f32[512,128]{1,0:T(8,128)S(1)}, u32[]{:S(2)}, u32[]{:S(2)}) %collective-permute-start.8) | collective-permute-done | bytes 262176 | tf_op jit(solution)/shard_map/ppermute | solution.py:173
  72.5 3.0 collective-permute-start.9
  75.5 1.9 collective-permute-start
  77.4 10.5 %collective-permute-done.9 = f32[512,128]{1,0:T(8,128)S(1)} collective-permute-done((f32[512,128]{1,0:T(8,128)S(1)}, f32[512,128]{1,0:T(8,128)S(1)}, u32[]{:S(2)}, u32[]{:S(2)}) %collective-permute-start.9) | collective-permute-done | bytes 262176 | tf_op jit(solution)/shard_map/ppermute | solution.py:173
  87.9 1.8 fusion
  89.7 1.9 collective-permute-start.10
  91.6 45.7 %collective-permute-done.10 = f32[512,128]{1,0:T(8,128)S(1)} collective-permute-done((f32[512,128]{1,0:T(8,128)S(1)}, f32[512,128]{1,0:T(8,128)S(1)}, u32[]{:S(2)}, u32[]{:S(2)}) %collective-permute-start.10) | collective-permute-done | bytes 262176 | tf_op jit(solution)/shard_map/ppermute | solution.py:173
  137.4 0.1 collective-permute-start.11
  137.5 6.4 %collective-permute-start.2 = (f32[512,512]{1,0:T(8,128)S(1)}, f32[512,512]{1,0:T(8,128)S(1)}, u32[]{:S(2)}, u32[]{:S(2)}) collective-permute-start(f32[512,512]{1,0:T(8,128)S(1)} %collective-permute-done.t0), channel_id=1, source_target_pairs={{0,2},{2,0},{1,3},{3,1},{4,6},{6,4},{5,7},{7,5},{8,10},{10,8},{9,1... | collective-permute-start | bytes 3145736 | tf_op jit(solution)/shard_map/ppermute | solution.py:173
  143.9 5.3 %collective-permute-done.11 = f32[512,128]{1,0:T(8,128)} collective-permute-done((f32[512,128]{1,0:T(8,128)S(1)}, f32[512,128]{1,0:T(8,128)}, u32[]{:S(2)}, u32[]{:S(2)}) %collective-permute-start.11) | collective-permute-done | bytes 262176 | tf_op jit(solution)/shard_map/ppermute | solution.py:173
  149.3 1.1 add.100
  150.4 0.6 convolution_multiply_fusion
  151.0 0.7 copy-done.6
  151.7 1.6 collective-permute-start.13
  153.3 16.3 %collective-permute-done.13 = f32[256,128]{1,0:T(8,128)S(1)} collective-permute-done((f32[256,128]{1,0:T(8,128)S(1)}, f32[256,128]{1,0:T(8,128)S(1)}, u32[]{:S(2)}, u32[]{:S(2)}) %collective-permute-start.13) | collective-permute-done | bytes 131104 | tf_op jit(solution)/shard_map/ppermute | solution.py:173
  169.6 0.9 dynamic-slice_add_fusion
  170.5 0.5 collective-permute-start.14
  171.1 6.9 %collective-permute-done.14 = f32[128,128]{1,0:T(8,128)S(1)} collective-permute-done((f32[128,128]{1,0:T(8,128)S(1)}, f32[128,128]{1,0:T(8,128)S(1)}, u32[]{:S(2)}, u32[]{:S(2)}) %collective-permute-start.14) | collective-permute-done | bytes 65568 | tf_op jit(solution)/shard_map/ppermute | solution.py:173
  178.0 0.8 collective-permute-start.15
  178.8 0.5 collective-permute-start.3
  179.3 3.5 %collective-permute-done.15 = f32[64,128]{1,0:T(8,128)S(1)} collective-permute-done((f32[64,128]{1,0:T(8,128)S(1)}, f32[64,128]{1,0:T(8,128)S(1)}, u32[]{:S(2)}, u32[]{:S(2)}) %collective-permute-start.15) | collective-permute-done | bytes 32800 | tf_op jit(solution)/shard_map/ppermute | solution.py:173
  182.8 0.1 collective-permute-start.16
  182.9 0.7 collective-permute-start.12
  183.6 4.5 %collective-permute-done.16 = f32[32,128]{1,0:T(8,128)S(1)} collective-permute-done((f32[32,128]{1,0:T(8,128)S(1)}, f32[32,128]{1,0:T(8,128)S(1)}, u32[]{:S(2)}, u32[]{:S(2)}) %collective-permute-start.16) | collective-permute-done | bytes 16416 | tf_op jit(solution)/shard_map/ppermute | solution.py:173
  188.2 0.6 pad_add_fusion.where_ref
  188.8 0.5 collective-permute-done.17
  189.3 0.6 dynamic-slice_add_fusion.4
  189.9 0.0 all-gather.3.cloned.1.call-done
  190.0 0.9 copy-done.3
  190.9 26.3 %gram_first.1 = (f32[4,512,512]{2,1,0:T(8,128)}, bf16[4,512,512]{2,1,0:T(8,128)(2,1)}, bf16[4,512,512]{2,1,0:T(8,128)(2,1)}) custom-call(s32[2]{0:T(128)} %pad_add_fusion.where_ref, f32[512,512]{1,0:T(8,128)} %copy-done.1, f32[512,512]{1,0:T(8,128)} %copy-done.3, f32[512,512]{1,0:T(8,128)} %copy-done.2, f32[512,512]{1,0:T(8,128)} %collective-permute-done.3.t3, ...), custom_call_target="tpu_custom_call" | custom-call | tf_op jit(solution)/shard_map/gram_first/pallas_call | solution.py:83
  217.3 56.4 %all-gather.5.cloned.1.call-done = f32[8192,512]{1,0:T(8,128)} async-done(((f32[512,512]{1,0:T(8,128)}), f32[8192,512]{1,0:T(8,128)}) %all-gather.5.cloned.1.call-update) | async-done | bytes 16777232 | tf_op jit(solution)/shard_map/all_gather | solution.py:210
  273.7 27.7 %gram_last.1 = f32[4096,512]{1,0:T(8,128)} custom-call(s32[2]{0:T(128)} %pad_add_fusion.where_ref, bf16[4,512,512]{2,1,0:T(8,128)(2,1)} %get-tuple-element.11.hi_ref, bf16[4,512,512]{2,1,0:T(8,128)(2,1)} %get-tuple-element.12.lo_ref, f32[4,512,512]{2,1,0:T(8,128)} %get-tuple-element.13.first_ref, f32[4,4,512,512]{3,2,1,0:T(8,128)} %bitcast.12), custom_call_target="tpu_custom_call" | custom-call | tf_op jit(solution)/shard_map/gram_last/pallas_call | solution.py:148
  301.4 0.6 copy.9
  (32 shorter events, 0.3 us)
Async XLA Ops:
  7.2 182.8 %all-gather.3.cloned.1.call-start = ((), (), s32[]{:S(2)}) async-start(), calls=%async_computation | async-start | bytes 17825792 | tf_op jit(solution)/shard_map/all_gather | solution.py:209
  11.5 138.9 %copy-start = (f32[512,512]{1,0:T(8,128)S(1)}, f32[512,512]{1,0:T(8,128)}, u32[]{:S(2)}) copy-start(f32[512,512]{1,0:T(8,128)} %get-tuple-element.10) | copy-start | bytes 3145732
  11.5 262.2 %all-gather.5.cloned.1.call-start = ((), (), s32[]{:S(2)}) async-start(), calls=%async_computation.1 | async-start | bytes 17825792 | tf_op jit(solution)/shard_map/all_gather | solution.py:210
  11.6 25.1 %collective-permute-start.4 = (f32[512,512]{1,0:T(8,128)}, f32[512,512]{1,0:T(8,128)S(1)}, u32[]{:S(2)}, u32[]{:S(2)}) collective-permute-start(f32[512,512]{1,0:T(8,128)} %get-tuple-element.10), channel_id=1, source_target_pairs={{0,16},{16,0},{1,17},{17,1},{2,18},{18,2},{3,19},{19,3},{4,20},{20... | collective-permute-start | bytes 3145736 | tf_op jit(solution)/shard_map/ppermute | solution.py:173
  36.7 1.0 copy-start.5
  37.7 1.8 collective-permute-start.5
  40.5 10.0 %collective-permute-start.6 = (f32[512,128]{1,0:T(8,128)S(1)}, f32[512,128]{1,0:T(8,128)S(1)}, u32[]{:S(2)}, u32[]{:S(2)}) collective-permute-start(f32[512,128]{1,0:T(8,128)S(1)} %add.94), channel_id=1, source_target_pairs={{0,2},{2,0},{1,3},{3,1},{4,6},{6,4},{5,7},{7,5},{8,10},{10,8},{9,1... | collective-permute-start | bytes 786440 | tf_op jit(solution)/shard_map/ppermute | solution.py:173
  50.6 7.7 %collective-permute-start.7 = (f32[512,128]{1,0:T(8,128)S(1)}, f32[512,128]{1,0:T(8,128)S(1)}, u32[]{:S(2)}, u32[]{:S(2)}) collective-permute-start(f32[512,128]{1,0:T(8,128)S(1)} %add.95), channel_id=1, source_target_pairs={{0,16},{16,0},{1,17},{17,1},{2,18},{18,2},{3,19},{19,3},{4,20},{20... | collective-permute-start | bytes 786440 | tf_op jit(solution)/shard_map/ppermute | solution.py:173
  58.3 14.1 %collective-permute-start.8 = (f32[512,128]{1,0:T(8,128)S(1)}, f32[512,128]{1,0:T(8,128)S(1)}, u32[]{:S(2)}, u32[]{:S(2)}) collective-permute-start(f32[512,128]{1,0:T(8,128)S(1)} %add.96), channel_id=1, source_target_pairs={{0,4},{4,0},{8,12},{12,8},{1,5},{5,1},{9,13},{13,9},{2,6},{6,2},{1... | collective-permute-start | bytes 786440 | tf_op jit(solution)/shard_map/ppermute | solution.py:173
  72.5 15.4 %collective-permute-start.9 = (f32[512,128]{1,0:T(8,128)S(1)}, f32[512,128]{1,0:T(8,128)S(1)}, u32[]{:S(2)}, u32[]{:S(2)}) collective-permute-start(f32[512,128]{1,0:T(8,128)S(1)} %add.97), channel_id=1, source_target_pairs={{0,8},{4,12},{8,0},{12,4},{1,9},{5,13},{9,1},{13,5},{2,10},{6,14},... | collective-permute-start | bytes 786440 | tf_op jit(solution)/shard_map/ppermute | solution.py:173
  75.5 62.0 %collective-permute-start = (f32[512,512]{1,0:T(8,128)}, f32[512,512]{1,0:T(8,128)S(1)}, u32[]{:S(2)}, u32[]{:S(2)}) collective-permute-start(f32[512,512]{1,0:T(8,128)} %get-tuple-element.9), channel_id=1, source_target_pairs={{0,0},{1,32},{2,64},{3,96},{32,1},{33,33},{34,65},{35,97},{64,2},{... | collective-permute-start | bytes 3145736 | tf_op jit(solution)/shard_map/ppermute | solution.py:177
  89.7 47.6 %collective-permute-start.10 = (f32[512,128]{1,0:T(8,128)S(1)}, f32[512,128]{1,0:T(8,128)S(1)}, u32[]{:S(2)}, u32[]{:S(2)}) collective-permute-start(f32[512,128]{1,0:T(8,128)S(1)} %fusion), channel_id=1, source_target_pairs={{0,32},{32,0},{64,96},{96,64},{1,33},{33,1},{65,97},{97,65},{2,34}... | collective-permute-start | bytes 786440 | tf_op jit(solution)/shard_map/ppermute | solution.py:173
  137.4 6.6 %copy-start.4 = (f32[512,128]{1,0:T(8,128)}, f32[512,128]{1,0:T(8,128)S(1)}, u32[]{:S(2)}) copy-start(f32[512,128]{1,0:T(8,128)S(1)} %add.99) | copy-start | bytes 786436
  137.4 11.9 %collective-permute-start.11 = (f32[512,128]{1,0:T(8,128)S(1)}, f32[512,128]{1,0:T(8,128)}, u32[]{:S(2)}, u32[]{:S(2)}) collective-permute-start(f32[512,128]{1,0:T(8,128)S(1)} %add.99), channel_id=1, source_target_pairs={{0,64},{32,96},{64,0},{96,32},{1,65},{33,97},{65,1},{97,33},{2,66}... | collective-permute-start | bytes 786440 | tf_op jit(solution)/shard_map/ppermute | solution.py:173
  137.5 52.5 %copy-start.1 = (f32[512,512]{1,0:T(8,128)}, f32[512,512]{1,0:T(8,128)S(1)}, u32[]{:S(2)}) copy-start(f32[512,512]{1,0:T(8,128)S(1)} %collective-permute-done.t0) | copy-start | bytes 3145732
  137.5 41.2 %collective-permute-start.2 = (f32[512,512]{1,0:T(8,128)S(1)}, f32[512,512]{1,0:T(8,128)S(1)}, u32[]{:S(2)}, u32[]{:S(2)}) collective-permute-start(f32[512,512]{1,0:T(8,128)S(1)} %collective-permute-done.t0), channel_id=1, source_target_pairs={{0,2},{2,0},{1,3},{3,1},{4,6},{6,4},{5,7},{7,5},{8,10},{10,8},{9,1... | collective-permute-start | bytes 3145736 | tf_op jit(solution)/shard_map/ppermute | solution.py:173
  150.9 0.7 copy-start.6
  151.7 17.9 %collective-permute-start.13 = (f32[256,128]{1,0:T(8,128)S(1)}, f32[256,128]{1,0:T(8,128)S(1)}, u32[]{:S(2)}, u32[]{:S(2)}) collective-permute-start(f32[256,128]{1,0:T(8,128)S(1)} %constant_dynamic-slice_fusion.4), channel_id=1, source_target_pairs={{0,16},{16,0},{1,17},{17,1},{2,18},{18,2},{3,19},{19,3},{4,20},{20... | collective-permute-start | bytes 393224 | tf_op jit(solution)/shard_map/ppermute | solution.py:173
  170.5 7.4 %collective-permute-start.14 = (f32[128,128]{1,0:T(8,128)S(1)}, f32[128,128]{1,0:T(8,128)S(1)}, u32[]{:S(2)}, u32[]{:S(2)}) collective-permute-start(f32[128,128]{1,0:T(8,128)S(1)} %constant_dynamic-slice_fusion.3), channel_id=1, source_target_pairs={{0,8},{4,12},{8,0},{12,4},{1,9},{5,13},{9,1},{13,5},{2,10},{6,14},... | collective-permute-start | bytes 196616 | tf_op jit(solution)/shard_map/ppermute | solution.py:173
  178.0 4.8 %collective-permute-start.15 = (f32[64,128]{1,0:T(8,128)S(1)}, f32[64,128]{1,0:T(8,128)S(1)}, u32[]{:S(2)}, u32[]{:S(2)}) collective-permute-start(f32[64,128]{1,0:T(8,128)S(1)} %constant_dynamic-slice_fusion.2), channel_id=1, source_target_pairs={{0,4},{4,0},{8,12},{12,8},{1,5},{5,1},{9,13},{13,9},{2,6},{6,2},{1... | collective-permute-start | bytes 98312 | tf_op jit(solution)/shard_map/ppermute | solution.py:173
  178.7 11.2 %collective-permute-start.1 = (f32[512,512]{1,0:T(8,128)S(1)}, f32[512,512]{1,0:T(8,128)S(1)}, u32[]{:S(2)}, u32[]{:S(2)}) collective-permute-start(f32[512,512]{1,0:T(8,128)S(1)} %collective-permute-done.t0), channel_id=1, source_target_pairs={{0,1},{1,0},{2,3},{3,2},{4,5},{5,4},{6,7},{7,6},{8,9},{9,8},{10,11... | collective-permute-start | bytes 3145736 | tf_op jit(solution)/shard_map/ppermute | solution.py:173
  178.7 11.2 %copy-start.2 = (f32[512,512]{1,0:T(8,128)}, f32[512,512]{1,0:T(8,128)S(1)}, u32[]{:S(2)}) copy-start(f32[512,512]{1,0:T(8,128)S(1)} %collective-permute-done.2.t2) | copy-start | bytes 3145732
  178.8 11.2 %collective-permute-start.3 = (f32[512,512]{1,0:T(8,128)S(1)}, f32[512,512]{1,0:T(8,128)}, u32[]{:S(2)}, u32[]{:S(2)}) collective-permute-start(f32[512,512]{1,0:T(8,128)S(1)} %collective-permute-done.2.t2), channel_id=1, source_target_pairs={{0,1},{1,0},{2,3},{3,2},{4,5},{5,4},{6,7},{7,6},{8,9},{9,8},{10,11... | collective-permute-start | bytes 3145736 | tf_op jit(solution)/shard_map/ppermute | solution.py:173
  182.8 5.3 %collective-permute-start.16 = (f32[32,128]{1,0:T(8,128)S(1)}, f32[32,128]{1,0:T(8,128)S(1)}, u32[]{:S(2)}, u32[]{:S(2)}) collective-permute-start(f32[32,128]{1,0:T(8,128)S(1)} %constant_dynamic-slice_fusion.1), channel_id=1, source_target_pairs={{0,2},{2,0},{1,3},{3,1},{4,6},{6,4},{5,7},{7,5},{8,10},{10,8},{9,1... | collective-permute-start | bytes 49160 | tf_op jit(solution)/shard_map/ppermute | solution.py:173
  182.9 5.9 %collective-permute-start.12 = (f32[128,128]{1,0:T(8,128)S(1)}, f32[128,128]{1,0:T(8,128)S(1)}, u32[]{:S(2)}, u32[]{:S(2)}) collective-permute-start(f32[128,128]{1,0:T(8,128)S(1)} %constant_dynamic-slice_fusion.5), channel_id=1, source_target_pairs={{0,0},{1,32},{2,64},{3,96},{32,1},{33,33},{34,65},{35,97},{64,2},{... | collective-permute-start | bytes 196616 | tf_op jit(solution)/shard_map/ppermute | solution.py:177
  188.1 1.2 collective-permute-start.17
  189.9 1.0 copy-start.3
Sparse Core Ops, SparseCore 0:
  11.6 146.1 all-gather.2
  159.9 113.7 all-gather.4
